TPU v7x, 32 devices: a whole 2x2x4 slice. The times are simulated.
32 devices in a mesh: groups: 2 (over y), seq: 4 (over z), tp: 4 (over x, core).
Axes of the slice: x: 2, y: 2, z: 4, core: 2. Of those that a mesh axis runs over, the one named last changes fastest.
Arguments:
- queries: bfloat16 [8, 128, 5120], P('groups', 'seq', 'tp'), parts along dimension 0, may hold values from -40 to 40
- key_vectors: bfloat16 [8, 128, 5120], P('groups', 'seq', 'tp'), parts along dimension 0, may hold values from -40 to 40
- value_vectors: bfloat16 [8, 128, 5120], P('groups', 'seq', 'tp'), parts along dimension 0, may hold values from -6 to 6
- block_mask: int32 [40, 4, 4], P('tp'), may hold values from 0 to 1, as said below
- out_weight: bfloat16 [40, 128, 2560], P('tp', 'seq'), may hold values from -0.5 to 0.5
Outputs:
- projected: bfloat16 [8, 128, 2560], P('groups', 'seq', 'tp'), parts along dimension 0
There are 2 independent parts, one for each index of `groups`. A program takes and returns all parts, laid end to end along the dimension named above; an argument that names none is the same for every part. Nothing has to cross between parts.
Inputs may be any that keep to these rules, and one draw needn't show every extreme that they name: block_mask[h, b, b] = 1 for every head and block; every row of a head's mask has at most 4 ones, and every head has a row with exactly 4.
All inputs are finite; a program needn't handle non-finite values.
Results may differ from a plain program's by a relative error of at most 0.012.
Values may be sent and summed in bfloat16 or wider, within the bound.
No kernel may reach another device: no remote copies, remote signals or barrier semaphores. Data moves between devices by JAX's collectives and lax.ppermute only.
A program may use at most 64 MiB of HBM per device.

v0:
```python
import jax
import jax.numpy as jnp
import numpy as np
from jax import lax
from jax.sharding import PartitionSpec as P

KEYS = 28


def strip_tables(heads_local, blocks, slot_total):
    slot_ids = np.arange(slot_total)
    head_of = slot_ids * heads_local // slot_total
    per_head = np.bincount(head_of, minlength=heads_local)
    head_begin = np.cumsum(per_head) - per_head
    order_in_head = slot_ids - head_begin[head_of]
    head_share = per_head[head_of]
    first_block = order_in_head * blocks // head_share
    block_count = (order_in_head + 1) * blocks // head_share - first_block
    return (head_of, first_block, block_count)


def body(queries, key_vectors, value_vectors, block_mask, out_weight):
    rank_count = lax.axis_size("seq")
    my_rank = lax.axis_index("seq")
    block_total, row_share, feature_width = queries.shape
    heads_local = block_mask.shape[0]
    head_size = feature_width // heads_local
    block_rows = row_share * rank_count
    per_rank = (heads_local + rank_count - 1) // rank_count
    slot_total = rank_count * per_rank
    least_share = slot_total // heads_local
    strip_cap = ((block_total + least_share - 1) // least_share + 1) // 2 * 2
    key_cap = min(KEYS, block_total)
    head_of, first_block, block_count = strip_tables(heads_local, block_total, slot_total)
    slot_grid = np.arange(slot_total).reshape(rank_count, per_rank).T
    paired = jnp.concatenate(
        [
            key_vectors.reshape(block_total, row_share, heads_local, head_size),
            value_vectors.reshape(block_total, row_share, heads_local, head_size),
        ],
        axis=3,
    )
    send_heads = jnp.asarray(head_of[slot_grid].reshape(-1), jnp.int32)
    chosen = jnp.take(paired, send_heads, axis=2)
    chosen = chosen.reshape(block_total, row_share, per_rank, rank_count, 2 * head_size)
    outgoing_pairs = chosen.transpose(2, 0, 3, 1, 4).reshape(
        per_rank, block_total, block_rows, 2 * head_size
    )
    flat_queries = queries.reshape(block_total, row_share, heads_local, head_size).transpose(
        0, 2, 1, 3
    )
    flat_queries = flat_queries.reshape(block_total * heads_local, row_share, head_size)
    positions = np.arange(strip_cap)
    unit_block = first_block[slot_grid][:, None, :] + positions[None, :, None]
    is_live = positions[None, :, None] < block_count[slot_grid][:, None, :]
    unit_index = np.where(is_live, unit_block * heads_local + head_of[slot_grid][:, None, :], 0)
    picked = jnp.take(flat_queries, jnp.asarray(unit_index.reshape(-1), jnp.int32), axis=0)
    picked = jnp.where(
        jnp.asarray(is_live.reshape(-1))[:, None, None], picked, jnp.zeros_like(picked)
    )
    outgoing_queries = picked.reshape(per_rank, strip_cap, block_rows, head_size)
    strip_queries, strip_pairs = (
        lax.all_to_all(outgoing_queries, "seq", split_axis=2, concat_axis=2, tiled=True),
        lax.all_to_all(outgoing_pairs, "seq", split_axis=2, concat_axis=2, tiled=True),
    )
    my_slots = my_rank * per_rank + jnp.arange(per_rank, dtype=jnp.int32)
    my_heads = jnp.asarray(head_of, jnp.int32)[my_slots]
    my_first = jnp.asarray(first_block, jnp.int32)[my_slots]
    query_blocks = jnp.minimum(
        my_first[:, None] + jnp.arange(strip_cap, dtype=jnp.int32)[None, :], block_total - 1
    )
    mask_rows = block_mask[my_heads[:, None], query_blocks]
    column_ids = jnp.arange(block_total, dtype=jnp.int32)
    ranking = (1 - mask_rows) * block_total + column_ids
    key_pick = jnp.argsort(ranking, axis=-1)[..., :key_cap]
    key_live = jnp.take_along_axis(mask_rows, key_pick, axis=-1)
    group_total = per_rank * strip_cap // 2
    query_groups = strip_queries.reshape(group_total, 2, block_rows, head_size)
    pick_groups = key_pick.reshape(group_total, 2, key_cap)
    live_groups = key_live.reshape(group_total, 2, key_cap)
    slot_of_group = jnp.arange(group_total, dtype=jnp.int32) // (strip_cap // 2)
    score_scale = head_size ** (-0.5)

    def attend_group(inputs):
        query_tile, pick_tile, live_tile, slot_index = inputs
        pairs_here = strip_pairs[slot_index]
        gathered = pairs_here[pick_tile]
        scores = (
            jnp.einsum(
                "qid,qkjd->qikj",
                query_tile,
                gathered[..., :head_size],
                preferred_element_type=jnp.float32,
            )
            * score_scale
        )
        allowed = (live_tile > 0)[:, None, :, None]
        scores = jnp.where(allowed, scores, -jnp.inf)
        largest = jnp.max(scores, axis=(2, 3), keepdims=True)
        weights = jnp.exp(scores - largest)
        totals = jnp.sum(weights, axis=(2, 3))
        blended = jnp.einsum(
            "qikj,qkjd->qid",
            weights.astype(jnp.bfloat16),
            gathered[..., head_size:],
            preferred_element_type=jnp.float32,
        )
        return (blended / totals[..., None]).astype(jnp.bfloat16)

    strip_out = lax.map(attend_group, (query_groups, pick_groups, live_groups, slot_of_group))
    outgoing_out = strip_out.reshape(per_rank, strip_cap, block_rows, head_size)
    returned = lax.all_to_all(outgoing_out, "seq", split_axis=2, concat_axis=2, tiled=True)
    slot_mesh, step_mesh = np.meshgrid(np.arange(slot_total), positions, indexing="ij")
    live_slot = step_mesh < block_count[slot_mesh]
    placement_index = np.zeros((block_total, heads_local), np.int64)
    source_index = (
        slot_mesh % per_rank * strip_cap + step_mesh
    ) * rank_count + slot_mesh // per_rank
    placement_index[
        first_block[slot_mesh][live_slot] + step_mesh[live_slot], head_of[slot_mesh][live_slot]
    ] = source_index[live_slot]
    flat_back = returned.reshape(per_rank * strip_cap * rank_count, row_share, head_size)
    own_out = jnp.take(flat_back, jnp.asarray(placement_index.reshape(-1), jnp.int32), axis=0)
    own_out = own_out.reshape(block_total, heads_local, row_share, head_size)
    token_total = block_total * row_share
    token_out = own_out.transpose(0, 2, 1, 3).reshape(token_total, heads_local, head_size)
    partial_sum = jnp.einsum(
        "thd,hdo->to",
        token_out,
        lax.all_gather(out_weight, "seq", axis=1, tiled=True),
        preferred_element_type=jnp.float32,
    )
    summed = lax.psum_scatter(
        partial_sum.astype(jnp.bfloat16), "tp", scatter_dimension=1, tiled=True
    ).astype(jnp.float32)
    return summed.astype(jnp.bfloat16).reshape(block_total, row_share, summed.shape[1])


def solution(mesh):
    return jax.shard_map(
        body,
        mesh=mesh,
        in_specs=(
            P("groups", "seq", "tp"),
            P("groups", "seq", "tp"),
            P("groups", "seq", "tp"),
            P("tp", None, None),
            P("tp", "seq", None),
        ),
        out_specs=P("groups", "seq", "tp"),
        check_vma=False,
    )
```

profile of v0, /device:TPU:0, one launch (start us, length us, event | category | flops | bytes accessed | tf_op | source)
XLA Modules:
  0.0 199.6 jit_solution(3571935745771503848)
XLA Ops:
  6.5 1.2 reshape.189
  8.6 1.6 copy_select_fusion
  10.2 6.5 %all-to-all-start = ((bf16[3,4,128,128]{3,1,0,2:T(4,128)(2,1)}), bf16[3,4,128,128]{3,1,0,2:T(4,128)(2,1)S(1)}, u32[]{:S(2)}, u32[]{:S(2)}) async-start(bf16[3,4,128,128]{3,1,0,2:T(4,128)(2,1)} %copy_select_fusion), calls=%async_computation | async-start | bytes 786432 | tf_op jit(solution)/shard_map/all_to_all | solution.py:63
  16.7 0.7 all-gather.2.cloned.1.call-update
  19.7 1.5 copy.76
  21.2 7.2 %all-to-all-done = bf16[3,4,128,128]{3,1,0,2:T(4,128)(2,1)S(1)} async-done(((bf16[3,4,128,128]{3,1,0,2:T(4,128)(2,1)}), bf16[3,4,128,128]{3,1,0,2:T(4,128)(2,1)S(1)}, u32[]{:S(2)}, u32[]{:S(2)}) %all-to-all-start) | async-done | bytes 393248 | tf_op jit(solution)/shard_map/all_to_all | solution.py:63
  28.4 3.5 %all-to-all-start.1 = ((bf16[3,4,128,256]{3,1,0,2:T(4,128)(2,1)}), bf16[3,4,128,256]{3,1,0,2:T(4,128)(2,1)S(1)}, u32[]{:S(2)}, u32[]{:S(2)}) async-start(bf16[3,4,128,256]{3,1,0,2:T(4,128)(2,1)} %copy.76), calls=%async_computation.1 | async-start | bytes 1572864 | tf_op jit(solution)/shard_map/all_to_all | solution.py:64
  33.0 1.3 sort.17
  34.6 1.2 gather_fusion.7
  36.1 36.5 %all-to-all-done.1 = bf16[3,4,128,256]{3,1,0,2:T(4,128)(2,1)S(1)} async-done(((bf16[3,4,128,256]{3,1,0,2:T(4,128)(2,1)}), bf16[3,4,128,256]{3,1,0,2:T(4,128)(2,1)S(1)}, u32[]{:S(2)}, u32[]{:S(2)}) %all-to-all-start.1) | async-done | bytes 786464 | tf_op jit(solution)/shard_map/all_to_all | solution.py:64
  72.6 30.0 %while.10 = (s32[]{:T(128)}, bf16[6,2,128,128]{3,1,0,2:T(2,128)(2,1)}, s32[6,2,4]{2,1,0:T(2,128)S(1)}, bf16[6,2,128,128]{3,1,0,2:T(2,128)(2,1)S(1)}, s32[6]{0:T(...) while((s32[]{:T(128)}, ...), condition=%wide.region_4.5_spmd, body=%wide.region_1.4_spmd.sunk | while | flops 68092448 | bytes 4598155 | solution.py:110
  76.9 0.7 copy_dynamic-update-slice_fusion.2
  81.9 0.7 copy_dynamic-update-slice_fusion.2
  86.9 0.7 copy_dynamic-update-slice_fusion.2
  91.9 0.7 copy_dynamic-update-slice_fusion.2
  96.9 0.7 copy_dynamic-update-slice_fusion.2
  101.9 0.7 copy_dynamic-update-slice_fusion.2
  102.6 3.5 %all-to-all-start.2 = ((bf16[3,4,128,128]{3,1,0,2:T(4,128)(2,1)}), bf16[3,4,128,128]{3,1,0,2:T(4,128)(2,1)S(1)}, u32[]{:S(2)}, u32[]{:S(2)}) async-start(bf16[3,4,128,128]{3,1,0,2:T(4,128)(2,1)} %bitcast.24), calls=%async_computation.2 | async-start | bytes 786432 | tf_op jit(solution)/shard_map/all_to_all | solution.py:112
  106.2 23.9 %all-to-all-done.2 = bf16[3,4,128,128]{3,1,0,2:T(4,128)(2,1)S(1)} async-done(((bf16[3,4,128,128]{3,1,0,2:T(4,128)(2,1)}), bf16[3,4,128,128]{3,1,0,2:T(4,128)(2,1)S(1)}, u32[]{:S(2)}, u32[]{:S(2)}) %all-to-all-start.2) | async-done | bytes 393248 | tf_op jit(solution)/shard_map/all_to_all | solution.py:112
  130.8 34.5 %all-gather.2.cloned.1.call-done = bf16[10,128,2560]{2,1,0:T(8,128)(2,1)} async-done(((bf16[10,32,2560]{2,1,0:T(8,128)(2,1)}), bf16[10,128,2560]{2,1,0:T(8,128)(2,1)}) %all-gather.2.cloned.1.call-update) | async-done | bytes 6553616 | tf_op jit(solution)/shard_map/all_gather | solution.py:130
  165.3 3.9 %fusion.11 = bf16[128,2560]{1,0:T(8,128)(2,1)S(1)} fusion(bf16[128,10,128]{2,0,1:T(8,128)(2,1)S(1)} %bitcast.102, bf16[10,128,2560]{2,1,0:T(8,128)(2,1)} %all-gather.2.cloned.1.call-done), kind=kOutput, calls=%fused_computation.32 | convolution fusion | flops 839188480 | bytes 7536640 | tf_op jit(solution)/shard_map/thd,hdo->to/dot_general | solution.py:127
  169.2 1.1 copy.86
  170.3 20.7 %reduce-scatter.4.cloned.1.call-done = bf16[640,128]{1,0:T(8,128)(2,1)} async-done(((bf16[2560,128]{1,0:T(8,128)(2,1)}), bf16[640,128]{1,0:T(8,128)(2,1)}) %reduce-scatter.4.cloned.1.call-update) | async-done | bytes 163856
  191.0 1.7 copy.87
  (130 shorter events, 18.5 us)
Async XLA Ops:
  6.5 12.2 %copy-start = (bf16[4,32,1280]{2,1,0:T(8,128)(2,1)S(1)}, bf16[4,32,1280]{2,1,0:T(8,128)(2,1)}, u32[]{:S(2)}) copy-start(bf16[4,32,1280]{2,1,0:T(8,128)(2,1)} %param.14) | copy-start | bytes 983044
  6.5 1.3 copy-start.8
  6.5 2.0 copy-start.5
  8.6 8.9 %copy-start.2 = (s32[12]{0:T(128)S(1)}, s32[12]{0:T(128)}, u32[]{:S(2)}) copy-start(s32[12]{0:T(128)} %constant.133.clone) | copy-start | bytes 148
  10.2 7.9 %copy-start.1 = (s32[12]{0:T(128)S(1)}, s32[12]{0:T(128)}, u32[]{:S(2)}) copy-start(s32[12]{0:T(128)} %constant.134.clone) | copy-start | bytes 148
  10.2 8.5 %copy-start.7 = (s32[12]{0:T(128)S(1)}, s32[12]{0:T(128)}, u32[]{:S(2)}) copy-start(s32[12]{0:T(128)} %constant.199) | copy-start | bytes 148
  10.2 8.6 %copy-start.3 = (bf16[4,32,1280]{2,1,0:T(8,128)(2,1)S(1)}, bf16[4,32,1280]{2,1,0:T(8,128)(2,1)}, u32[]{:S(2)}) copy-start(bf16[4,32,1280]{2,1,0:T(8,128)(2,1)} %param.15) | copy-start | bytes 983044
  10.2 18.2 %all-to-all-start = ((bf16[3,4,128,128]{3,1,0,2:T(4,128)(2,1)}), bf16[3,4,128,128]{3,1,0,2:T(4,128)(2,1)S(1)}, u32[]{:S(2)}, u32[]{:S(2)}) async-start(bf16[3,4,128,128]{3,1,0,2:T(4,128)(2,1)} %copy_select_fusion), calls=%async_computation | async-start | bytes 786432 | tf_op jit(solution)/shard_map/all_to_all | solution.py:63
  16.7 148.6 %all-gather.2.cloned.1.call-start = ((), (), s32[]{:S(2)}) async-start(), calls=%async_computation.4 | async-start | bytes 8192000 | tf_op jit(solution)/shard_map/all_gather | solution.py:130
  19.7 12.4 %copy-start.4 = (s32[10,4,4]{0,2,1:T(4,128)S(1)}, s32[10,4,4]{0,2,1:T(4,128)}, u32[]{:S(2)}) copy-start(s32[10,4,4]{0,2,1:T(4,128)} %param.16) | copy-start | bytes 1924
  28.4 44.2 %all-to-all-start.1 = ((bf16[3,4,128,256]{3,1,0,2:T(4,128)(2,1)}), bf16[3,4,128,256]{3,1,0,2:T(4,128)(2,1)S(1)}, u32[]{:S(2)}, u32[]{:S(2)}) async-start(bf16[3,4,128,256]{3,1,0,2:T(4,128)(2,1)} %copy.76), calls=%async_computation.1 | async-start | bytes 1572864 | tf_op jit(solution)/shard_map/all_to_all | solution.py:64
  72.6 33.5 %copy-start.6 = (s32[40]{0:T(128)S(1)}, s32[40]{0:T(128)}, u32[]{:S(2)}) copy-start(s32[40]{0:T(128)} %constant.200) | copy-start | bytes 484
  102.6 27.5 %all-to-all-start.2 = ((bf16[3,4,128,128]{3,1,0,2:T(4,128)(2,1)}), bf16[3,4,128,128]{3,1,0,2:T(4,128)(2,1)S(1)}, u32[]{:S(2)}, u32[]{:S(2)}) async-start(bf16[3,4,128,128]{3,1,0,2:T(4,128)(2,1)} %bitcast.24), calls=%async_computation.2 | async-start | bytes 786432 | tf_op jit(solution)/shard_map/all_to_all | solution.py:112
  106.1 84.9 %reduce-scatter.4.cloned.1.call-start = ((), (), s32[]{:S(2)}) async-start(), calls=%async_computation.5 | async-start | bytes 819200
Sparse Core Ops, SparseCore 0:
  19.1 146.1 all-gather.1
  170.4 20.5 reduce-scatter.3
where the time goes:
time: 200 us
  waiting for transfers between devices  124 us (62%)
  local copies, waits for them, and re-layouts  25.2 us (13%)
  between operations  13.7 us (7%)
  starting transfers between devices  13.5 us (7%)
  loops' own time  12.7 us (6%)
  matrix products  7.13 us (4%)
  other arithmetic  3.88 us (2%)
    all_to_all x1, waiting for transfers between devices, body(): lax.all_to_all(outgoing_pairs, 'seq', split_axis=2, concat_axis=2, tiled=...  36.5 us
    all_gather x1, waiting for transfers between devices, body(): lax.all_gather(out_weight, 'seq', axis=1, tiled=True)  34.5 us
    all_to_all x1, waiting for transfers between devices, body(): lax.all_to_all(outgoing_out, 'seq', split_axis=2, concat_axis=2, tiled=True)  23.9 us
    unnamed x3, waiting for transfers between devices  21.5 us
    another operation x1, loops' own time, body(): lax.map(attend_group, (query_groups, pick_groups, live_groups, slot_of_gr...  12.7 us
    all_to_all x1, waiting for transfers between devices, body(): lax.all_to_all(outgoing_queries, 'seq', split_axis=2, concat_axis=2, tile...  7.18 us
    all_to_all x1, starting transfers between devices, body(): lax.all_to_all(outgoing_queries, 'seq', split_axis=2, concat_axis=2, tile...  6.48 us
    dynamic_slice x12, local copies, waits for them, and re-layouts, body(): lax.map(attend_group, (query_groups, pick_groups, live_groups, slot_of_gr...  4.29 us
  transfers between devices with their start and end apart: 5, of which 5 were waited for; matrix products, arithmetic and copies ran while one was open for 13% of the time, Pallas kernels for 0%

commit v1 on v0

--- a/solution.py
+++ b/solution.py
@@ -3,6 +3,7 @@
 import numpy as np
 from jax import lax
 from jax.sharding import PartitionSpec as P
+from jax.lax import axis_index, ppermute, psum
 
 KEYS = 28
 
@@ -59,9 +60,23 @@
         jnp.asarray(is_live.reshape(-1))[:, None, None], picked, jnp.zeros_like(picked)
     )
     outgoing_queries = picked.reshape(per_rank, strip_cap, block_rows, head_size)
+
+    def proceed_the_indices(ndim_at, matrix, d_out=2):
+        odd, outer = (psum(1, "seq"), axis_index("seq"))
+        carry_out = matrix.shape[d_out] // odd
+        raw_out = jnp.roll(matrix, -outer * carry_out, d_out)
+        buffers = [lax.slice_in_dim(raw_out, 0, carry_out, axis=d_out)]
+        for to_i in range(1, odd):
+            k_now = lax.slice_in_dim(raw_out, to_i * carry_out, (to_i + 1) * carry_out, axis=d_out)
+            buffers.append(
+                ppermute(k_now, "seq", [(src_i, (src_i + to_i) % odd) for src_i in range(odd)])
+            )
+        fresh = jnp.concatenate(buffers[::-1], ndim_at)
+        return jnp.roll(fresh, (outer + 1) * buffers[0].shape[ndim_at], ndim_at)
+
     strip_queries, strip_pairs = (
         lax.all_to_all(outgoing_queries, "seq", split_axis=2, concat_axis=2, tiled=True),
-        lax.all_to_all(outgoing_pairs, "seq", split_axis=2, concat_axis=2, tiled=True),
+        proceed_the_indices(2, matrix=outgoing_pairs),
     )
     my_slots = my_rank * per_rank + jnp.arange(per_rank, dtype=jnp.int32)
     my_heads = jnp.asarray(head_of, jnp.int32)[my_slots]

time: 200 us -> 193 us (0.965)
  waiting for transfers between devices: 124 us -> 103 us
  starting transfers between devices: 13.5 us -> 28.3 us
  other arithmetic: 3.88 us -> 6.21 us
  local copies, waits for them, and re-layouts: 25.2 us -> 23.1 us
    all_to_all x1 -> x0, waiting for transfers between devices: 36.5 us -> none  [body(): lax.all_to_all(outgoing_pairs, 'seq', split_axis=2, concat_axis=2, tiled=...]
    all_to_all x1, starting transfers between devices: 3.46 us -> 17.8 us  [body(): lax.all_to_all(outgoing_out, 'seq', split_axis=2, concat_axis=2, tiled=True)]
    all_gather x1, waiting for transfers between devices: 34.5 us -> 47.6 us  [body(): lax.all_gather(out_weight, 'seq', axis=1, tiled=True)]
    ppermute x0 -> x3, waiting for transfers between devices: none -> 7.48 us  [proceed_the_indices(): ppermute(k_now, 'seq', [(src_i, (src_i + to_i) % odd) for src_i in range(...]
    ppermute x0 -> x3, starting transfers between devices: none -> 6.25 us  [proceed_the_indices(): ppermute(k_now, 'seq', [(src_i, (src_i + to_i) % odd) for src_i in range(...]
    all_to_all x1, waiting for transfers between devices: 7.18 us -> 2.13 us  [body(): lax.all_to_all(outgoing_queries, 'seq', split_axis=2, concat_axis=2, tile...]
    all_to_all x1 -> x0, starting transfers between devices: 3.51 us -> none  [body(): lax.all_to_all(outgoing_pairs, 'seq', split_axis=2, concat_axis=2, tiled=...]
    all_to_all x1, waiting for transfers between devices: 23.9 us -> 20.8 us  [body(): lax.all_to_all(outgoing_out, 'seq', split_axis=2, concat_axis=2, tiled=True)]
  transfers between devices with their start and end apart: 5 -> 7, of which waited for: 5 -> 5; matrix products, arithmetic and copies ran while one was open for 13% -> 14% of each run, Pallas kernels for 0% -> 0%
where the time goes in v1:
time: 193 us; the launch traced here: 192 us
  waiting for transfers between devices  103 us (53%)
  starting transfers between devices  28.3 us (15%)
  local copies, waits for them, and re-layouts  23.1 us (12%)
  between operations  13.6 us (7%)
  loops' own time  11.3 us (6%)
  matrix products  7.14 us (4%)
  other arithmetic  6.21 us (3%)
    all_gather x1, waiting for transfers between devices, body(): lax.all_gather(out_weight, 'seq', axis=1, tiled=True)  47.6 us
    unnamed x3, waiting for transfers between devices  24.5 us
    all_to_all x1, waiting for transfers between devices, body(): lax.all_to_all(outgoing_out, 'seq', split_axis=2, concat_axis=2, tiled=True)  20.8 us
    all_to_all x1, starting transfers between devices, body(): lax.all_to_all(outgoing_out, 'seq', split_axis=2, concat_axis=2, tiled=True)  17.8 us
    another operation x1, loops' own time, body(): lax.map(attend_group, (query_groups, pick_groups, live_groups, slot_of_gr...  11.3 us
    ppermute x3, waiting for transfers between devices, proceed_the_indices(): ppermute(k_now, 'seq', [(src_i, (src_i + to_i) % odd) for src_i in range(...  7.48 us
    ppermute x3, starting transfers between devices, proceed_the_indices(): ppermute(k_now, 'seq', [(src_i, (src_i + to_i) % odd) for src_i in range(...  6.25 us
    dynamic_update_slice x6, local copies, waits for them, and re-layouts, body(): lax.map(attend_group, (query_groups, pick_groups, live_groups, slot_of_gr...  4.27 us
  transfers between devices with their start and end apart: 7, of which 5 were waited for; matrix products, arithmetic and copies ran while one was open for 14% of the time, Pallas kernels for 0%

profile of v1, /device:TPU:0, one launch (start us, length us, event | category | flops | bytes accessed | tf_op | source)
XLA Modules:
  0.0 192.2 jit_solution(10101789413353211658)
XLA Ops:
  6.5 0.7 pad_clamp_fusion.2
  7.5 1.1 copy_bitcast_fusion.2
  9.9 5.1 %collective-permute-start = (bf16[3,4,32,256]{3,2,1,0:T(8,128)(2,1)S(1)}, bf16[3,4,32,256]{3,2,1,0:T(8,128)(2,1)S(1)}, u32[]{:S(2)}, u32[]{:S(2)}) collective-permute-start(bf16[3,4,32,256]{3,2,1,0:T(8,128)(2,1)S(1)} %copy.95), channel_id=1, source_target_pairs={{0,12},{4,0},{8,4},{12,8},{1,13},{5,1},{9,5},{13,9},{2,14},{6,2},{... | collective-permute-start | bytes 589832 | tf_op jit(solution)/shard_map/ppermute | solution.py:72
  15.1 1.0 collective-permute-start.2
  17.2 1.6 copy_select_fusion
  18.8 4.2 %all-to-all-start = ((bf16[3,4,128,128]{3,1,0,2:T(4,128)(2,1)}), bf16[3,4,128,128]{3,1,0,2:T(4,128)(2,1)S(1)}, u32[]{:S(2)}, u32[]{:S(2)}) async-start(bf16[3,4,128,128]{3,1,0,2:T(4,128)(2,1)} %copy_select_fusion), calls=%async_computation | async-start | bytes 786432 | tf_op jit(solution)/shard_map/all_to_all | solution.py:78
  23.1 0.7 all-gather.2.cloned.1.call-update
  26.3 1.3 sort.17
  27.7 1.2 gather_fusion.7
  29.4 7.5 %collective-permute-done.1 = bf16[3,4,32,256]{3,2,1,0:T(8,128)(2,1)S(1)} collective-permute-done((bf16[3,4,32,256]{3,2,1,0:T(8,128)(2,1)S(1)}, bf16[3,4,32,256]{3,2,1,0:T(8,128)(2,1)S(1)}, u32[]{:S(2)}, u32[]{:S(2)}) %collective-permute-start.1) | collective-permute-done | bytes 196640 | tf_op jit(solution)/shard_map/ppermute | solution.py:72
  36.9 1.3 fusion.15
  38.1 2.1 %all-to-all-done = bf16[3,4,128,128]{3,1,0,2:T(4,128)(2,1)S(1)} async-done(((bf16[3,4,128,128]{3,1,0,2:T(4,128)(2,1)}), bf16[3,4,128,128]{3,1,0,2:T(4,128)(2,1)S(1)}, u32[]{:S(2)}, u32[]{:S(2)}) %all-to-all-start) | async-done | bytes 393248 | tf_op jit(solution)/shard_map/all_to_all | solution.py:78
  40.3 27.7 %while.10 = (s32[]{:T(128)}, bf16[6,2,128,128]{3,1,0,2:T(2,128)(2,1)}, s32[6,2,4]{2,1,0:T(2,128)S(1)}, bf16[6,2,128,128]{3,1,0,2:T(2,128)(2,1)S(1)}, s32[6]{0:T(...) while((s32[]{:T(128)}, ...), condition=%wide.region_4.6_spmd, body=%wide.region_1.0_spmd.sunk | while | flops 68092448 | bytes 4073867 | solution.py:125
  48.8 0.7 copy_dynamic-update-slice_fusion.2
  53.4 0.7 copy_dynamic-update-slice_fusion.2
  62.6 0.7 copy_dynamic-update-slice_fusion.2
  67.2 0.7 copy_dynamic-update-slice_fusion.2
  67.9 17.8 %all-to-all-start.1 = ((bf16[3,4,128,128]{3,1,0,2:T(4,128)(2,1)}), bf16[3,4,128,128]{3,1,0,2:T(4,128)(2,1)S(1)}, u32[]{:S(2)}, u32[]{:S(2)}) async-start(bf16[3,4,128,128]{3,1,0,2:T(4,128)(2,1)} %bitcast.26), calls=%async_computation.1 | async-start | bytes 786432 | tf_op jit(solution)/shard_map/all_to_all | solution.py:127
  85.7 20.8 %all-to-all-done.1 = bf16[3,4,128,128]{3,1,0,2:T(4,128)(2,1)S(1)} async-done(((bf16[3,4,128,128]{3,1,0,2:T(4,128)(2,1)}), bf16[3,4,128,128]{3,1,0,2:T(4,128)(2,1)S(1)}, u32[]{:S(2)}, u32[]{:S(2)}) %all-to-all-start.1) | async-done | bytes 393248 | tf_op jit(solution)/shard_map/all_to_all | solution.py:127
  107.3 47.6 %all-gather.2.cloned.1.call-done = bf16[10,128,2560]{2,1,0:T(8,128)(2,1)} async-done(((bf16[10,32,2560]{2,1,0:T(8,128)(2,1)}), bf16[10,128,2560]{2,1,0:T(8,128)(2,1)}) %all-gather.2.cloned.1.call-update) | async-done | bytes 6553616 | tf_op jit(solution)/shard_map/all_gather | solution.py:145
  154.9 3.9 %fusion.11 = bf16[128,2560]{1,0:T(8,128)(2,1)S(1)} fusion(bf16[128,10,128]{2,0,1:T(8,128)(2,1)S(1)} %bitcast.100, bf16[10,128,2560]{2,1,0:T(8,128)(2,1)} %all-gather.2.cloned.1.call-done), kind=kOutput, calls=%fused_computation.31 | convolution fusion | flops 839188480 | bytes 7536640 | tf_op jit(solution)/shard_map/thd,hdo->to/dot_general | solution.py:142
  158.8 1.1 copy.89
  159.9 23.7 %reduce-scatter.4.cloned.1.call-done = bf16[640,128]{1,0:T(8,128)(2,1)} async-done(((bf16[2560,128]{1,0:T(8,128)(2,1)}), bf16[640,128]{1,0:T(8,128)(2,1)}) %reduce-scatter.4.cloned.1.call-update) | async-done | bytes 163856
  183.7 1.7 copy.90
  (131 shorter events, 19.9 us)
Async XLA Ops:
  6.5 1.0 copy-start
  9.8 6.4 %copy-start.3 = (bf16[4,32,1280]{2,1,0:T(8,128)(2,1)S(1)}, bf16[4,32,1280]{2,1,0:T(8,128)(2,1)}, u32[]{:S(2)}) copy-start(bf16[4,32,1280]{2,1,0:T(8,128)(2,1)} %param.15) | copy-start | bytes 983044
  9.8 6.6 %copy-start.7 = (s32[48]{0:T(128)S(1)}, s32[48]{0:T(128)}, u32[]{:S(2)}) copy-start(s32[48]{0:T(128)} %constant.218) | copy-start | bytes 580
  9.9 19.5 %collective-permute-start = (bf16[3,4,32,256]{3,2,1,0:T(8,128)(2,1)S(1)}, bf16[3,4,32,256]{3,2,1,0:T(8,128)(2,1)S(1)}, u32[]{:S(2)}, u32[]{:S(2)}) collective-permute-start(bf16[3,4,32,256]{3,2,1,0:T(8,128)(2,1)S(1)} %copy.95), channel_id=1, source_target_pairs={{0,12},{4,0},{8,4},{12,8},{1,13},{5,1},{9,5},{13,9},{2,14},{6,2},{... | collective-permute-start | bytes 589832 | tf_op jit(solution)/shard_map/ppermute | solution.py:72
  15.0 2.1 %copy-start.5 = (pred[3,4,4]{1,0,2:T(4,128)(4,1)S(1)}, pred[3,4,4]{1,0,2:T(4,128)(4,1)}, u32[]{:S(2)}) copy-start(pred[3,4,4]{1,0,2:T(4,128)(4,1)} %constant.165) | copy-start | bytes 148
  15.0 21.8 %collective-permute-start.1 = (bf16[3,4,32,256]{3,2,1,0:T(8,128)(2,1)S(1)}, bf16[3,4,32,256]{3,2,1,0:T(8,128)(2,1)S(1)}, u32[]{:S(2)}, u32[]{:S(2)}) collective-permute-start(bf16[3,4,32,256]{3,2,1,0:T(8,128)(2,1)S(1)} %copy.96), channel_id=1, source_target_pairs={{0,8},{4,12},{8,0},{12,4},{1,9},{5,13},{9,1},{13,5},{2,10},{6,14},... | collective-permute-start | bytes 589832 | tf_op jit(solution)/shard_map/ppermute | solution.py:72
  15.1 21.7 %collective-permute-start.2 = (bf16[3,4,32,256]{3,2,1,0:T(8,128)(2,1)S(1)}, bf16[3,4,32,256]{3,2,1,0:T(8,128)(2,1)S(1)}, u32[]{:S(2)}, u32[]{:S(2)}) collective-permute-start(bf16[3,4,32,256]{3,2,1,0:T(8,128)(2,1)S(1)} %copy.97), channel_id=1, source_target_pairs={{0,4},{4,8},{8,12},{12,0},{1,5},{5,9},{9,13},{13,1},{2,6},{6,10},{... | collective-permute-start | bytes 589832 | tf_op jit(solution)/shard_map/ppermute | solution.py:72
  17.2 6.6 %copy-start.2 = (s32[12]{0:T(128)S(1)}, s32[12]{0:T(128)}, u32[]{:S(2)}) copy-start(s32[12]{0:T(128)} %constant.153.clone) | copy-start | bytes 148
  18.8 5.6 %copy-start.1 = (s32[12]{0:T(128)S(1)}, s32[12]{0:T(128)}, u32[]{:S(2)}) copy-start(s32[12]{0:T(128)} %constant.154.clone) | copy-start | bytes 148
  18.8 6.5 %copy-start.4 = (s32[10,4,4]{0,2,1:T(4,128)S(1)}, s32[10,4,4]{0,2,1:T(4,128)}, u32[]{:S(2)}) copy-start(s32[10,4,4]{0,2,1:T(4,128)} %param.18) | copy-start | bytes 1924
  18.8 21.4 %all-to-all-start = ((bf16[3,4,128,128]{3,1,0,2:T(4,128)(2,1)}), bf16[3,4,128,128]{3,1,0,2:T(4,128)(2,1)S(1)}, u32[]{:S(2)}, u32[]{:S(2)}) async-start(bf16[3,4,128,128]{3,1,0,2:T(4,128)(2,1)} %copy_select_fusion), calls=%async_computation | async-start | bytes 786432 | tf_op jit(solution)/shard_map/all_to_all | solution.py:78
  23.1 131.9 %all-gather.2.cloned.1.call-start = ((), (), s32[]{:S(2)}) async-start(), calls=%async_computation.3 | async-start | bytes 8192000 | tf_op jit(solution)/shard_map/all_gather | solution.py:145
  40.3 45.4 %copy-start.6 = (s32[40]{0:T(128)S(1)}, s32[40]{0:T(128)}, u32[]{:S(2)}) copy-start(s32[40]{0:T(128)} %constant.220) | copy-start | bytes 484
  67.9 38.6 %all-to-all-start.1 = ((bf16[3,4,128,128]{3,1,0,2:T(4,128)(2,1)}), bf16[3,4,128,128]{3,1,0,2:T(4,128)(2,1)S(1)}, u32[]{:S(2)}, u32[]{:S(2)}) async-start(bf16[3,4,128,128]{3,1,0,2:T(4,128)(2,1)} %bitcast.26), calls=%async_computation.1 | async-start | bytes 786432 | tf_op jit(solution)/shard_map/all_to_all | solution.py:127
  85.7 98.0 %reduce-scatter.4.cloned.1.call-start = ((), (), s32[]{:S(2)}) async-start(), calls=%async_computation.4 | async-start | bytes 819200
Sparse Core Ops, SparseCore 0:
  25.4 129.4 all-gather.1
  160.0 23.5 reduce-scatter.3
